TPU v7x, 32 devices: a whole 2x2x4 slice. The times are simulated.
32 devices in a mesh: feat: 8 (over z, core), col: 4 (over y, x).
Axes of the slice: x: 2, y: 2, z: 4, core: 2. Of those that a mesh axis runs over, the one named last changes fastest.
Arguments:
- self_feats: bfloat16 [4096, 128], P(('feat', 'col')), may hold values from -6 to 6
- neighbour_feats: bfloat16 [128, 16384], P('feat', 'col'), may hold values from -6 to 6
- tiles: bfloat16 [1024, 128, 128], P('col'), may hold values from 0 to 1, as said below
- tile_rows: int32 [1024], P('col'), may hold values from 0 to 31, as said below
- tile_cols: int32 [1024], P('col'), may hold values from 0 to 31
- tile_count: int32 [4], P('col'), may hold values from 1 to 256, 768 in all
- owner_order: int32 [32], replicated, may hold values from 0 to 31, as said below
- degree: int32 [4096], P(('feat', 'col')), may hold values from 64 to 192
- w_self: bfloat16 [128, 256], replicated, may hold values from -0.5 to 0.5
- w_neigh: bfloat16 [128, 256], replicated, may hold values from -0.5 to 0.5
- bias: float32 [256], replicated, may hold values from -3 to 3
- upstream: bfloat16 [4096, 256], P(('feat', 'col')), may hold values from -6 to 6
Outputs:
- hidden_out: bfloat16 [4096, 256], P(('feat', 'col'))
- neigh_grad: bfloat16 [128, 16384], P('feat', 'col')
Inputs may be any that keep to these rules, and one draw needn't show every extreme that they name: `tiles`: every entry is 0 or 1. `tile_count`: slots at or after a group's count are ignored; some group has all 256 slots live. `owner_order`: a permutation of the row blocks. `tile_rows`: in every column group, slot s has a row block whose owner position p satisfies (p) % 4 == s % 4.
All inputs are finite; a program needn't handle non-finite values.
Results may differ from a plain program's by a relative error of at most 0.0065.
Values may be sent and summed in bfloat16 or wider, within the bound.
No kernel may reach another device: no remote copies, remote signals or barrier semaphores. Data moves between devices by JAX's collectives and lax.ppermute only.
A program may use at most 64 MiB of HBM per device.

v0:
```python
import jax
import jax.numpy as jnp
from jax import lax
from jax.sharding import PartitionSpec as P


def local(
    self_feats,
    neighbour_feats,
    tiles,
    tile_rows,
    tile_cols,
    tile_count,
    owner_order,
    degree,
    w_self,
    w_neigh,
    bias,
    upstream,
):
    nfeat = lax.axis_size("feat")
    ncol = lax.axis_size("col")
    slots, tile_size, _ = tiles.shape
    slice_width = neighbour_feats.shape[0]
    col_blocks = neighbour_feats.shape[1] // tile_size
    row_blocks = self_feats.shape[0] // tile_size
    blocks_total = owner_order.shape[0]
    places = (
        jnp.zeros((blocks_total,), jnp.int32)
        .at[owner_order]
        .set(jnp.arange(blocks_total, dtype=jnp.int32))
    )
    target = places[tile_rows]
    live = (jnp.arange(slots, dtype=jnp.int32) < tile_count[0]).astype(jnp.float32)
    blocked = neighbour_feats.reshape(slice_width, col_blocks, tile_size).transpose(1, 0, 2)
    picked = blocked[tile_cols]
    products = (
        jnp.einsum("nfk,nrk->nfr", picked, tiles, preferred_element_type=jnp.float32)
        * live[:, None, None]
    )
    partial_value = (
        jnp.zeros((blocks_total, slice_width, tile_size), jnp.float32).at[target].add(products)
    )
    grid = partial_value.reshape(nfeat, ncol, row_blocks, slice_width, tile_size)
    total = lax.psum(grid, "col")
    mine = lax.dynamic_slice_in_dim(total, lax.axis_index("col"), 1, 1)
    owned = lax.all_to_all(mine, "feat", split_axis=0, concat_axis=1, tiled=True)
    summed = owned.reshape(nfeat, row_blocks, slice_width, tile_size).transpose(1, 3, 0, 2)
    summed = summed.reshape(row_blocks * tile_size, nfeat * slice_width)
    scale = lax.rsqrt(degree.astype(jnp.float32))[:, None]
    aggregate = (summed * scale).astype(jnp.bfloat16)
    pre = jnp.dot(self_feats, w_self, preferred_element_type=jnp.float32)
    pre = pre + jnp.dot(aggregate, w_neigh, preferred_element_type=jnp.float32) + bias
    gate = jax.nn.sigmoid(pre)
    hidden_out = (pre * gate).astype(jnp.bfloat16)
    slope = gate * (1.0 + pre * (1.0 - gate))
    dpre = (upstream.astype(jnp.float32) * slope).astype(jnp.bfloat16)
    dagg = lax.dot_general(
        dpre, w_neigh, (((1,), (1,)), ((), ())), preferred_element_type=jnp.float32
    )
    back = (dagg * scale).astype(jnp.bfloat16)
    arranged = back.reshape(row_blocks, tile_size, nfeat, slice_width).transpose(2, 0, 3, 1)
    arranged = arranged.reshape(nfeat, 1, row_blocks, slice_width, tile_size)
    regrouped = lax.all_to_all(arranged, "feat", split_axis=0, concat_axis=0, tiled=True)
    everything = lax.all_gather(regrouped, "col", axis=1, tiled=True)
    row_grads = everything.reshape(blocks_total, slice_width, tile_size)
    taken = row_grads[target]
    pieces = (
        jnp.einsum("nfr,nrk->nfk", taken, tiles, preferred_element_type=jnp.float32)
        * live[:, None, None]
    )
    onehot_cols = (tile_cols[:, None] == jnp.arange(col_blocks, dtype=jnp.int32)[None, :]).astype(
        jnp.float32
    )
    col_total = jnp.einsum("nc,nfk->fck", onehot_cols, pieces, precision=lax.Precision.HIGHEST)
    neigh_grad = col_total.reshape(slice_width, col_blocks * tile_size).astype(jnp.bfloat16)
    return (hidden_out, neigh_grad)


def solution(mesh):
    in_specs = (
        P(("feat", "col"), None),
        P("feat", "col"),
        P("col", None, None),
        P("col"),
        P("col"),
        P("col"),
        P(),
        P(("feat", "col")),
        P(),
        P(),
        P(),
        P(("feat", "col"), None),
    )
    out_specs = (P(("feat", "col"), None), P("feat", "col"))
    return jax.shard_map(local, mesh=mesh, in_specs=in_specs, out_specs=out_specs, check_vma=False)
```

profile of v0, /device:TPU:0, one launch (start us, length us, event | category | flops | bytes accessed | tf_op | source)
XLA Modules:
  0.0 141.6 jit_solution(16048866213782390295)
XLA Ops:
  7.2 0.0 copy-start
  7.2 0.0 all-reduce.2.cloned.1.call-start
  7.2 0.7 compare_select_fusion.3
  7.9 0.7 scatter_custom_fusion
  8.6 0.7 fusion.14
  9.3 0.7 fusion.15
  10.0 20.7 %compare_select_fusion.4 = s32[256]{0:T(256)S(1)} fusion(s32[256]{0:T(256)} %param.15, s32[]{:T(128)} %bitcast, s32[]{:T(128)} %bitcast.1, s32[]{:T(128)} %bitcast.2, s32[]{:T(128)} %bitcast.3, s32[]{:T(128)} %bitcast.4, s32[]{:T(128)} %bitcast.5, s32[]{:T(128)} %bitcast.6, s32[]{:T(128)} %bitcast.7, s32[]{:T(128)} %bitcast.8, s32[]{:T(128)} %bitcast.9, ...), kind=kLoop, calls=%fused_computation.30 | loop fusion | flops 16640 | bytes 2176 | tf_op jit(solution)/shard_map/gather | solution.py:33
  31.5 0.7 compare_select_fusion.1
  32.2 0.8 gather_fusion
  33.0 6.8 %convolution_multiply_fusion.1 = f32[256,16,128]{2,1,0:T(8,128)S(1)} fusion(bf16[256,16,128]{2,1,0:T(8,128)(2,1)S(1)} %gather_fusion, bf16[256,128,128]{2,1,0:T(8,128)(2,1)} %param.14, f32[256]{0:T(256)S(1)} %compare_convert_fusion), kind=kOutput, calls=%fused_computation.7 | convolution fusion | flops 134742016 | bytes 11535360 | tf_op jit(solution)/shard_map/nfk,nrk->nfr/dot_general | solution.py:38
  39.9 0.0 copy-start.2
  39.9 0.0 copy-start.3
  39.9 0.0 copy-start.5
  39.9 0.0 copy-start.7
  39.9 9.0 %scatter_fusion = f32[32,16,128]{2,1,0:T(8,128)S(1)} fusion(f32[32,16,128]{2,1,0:T(8,128)S(1)} %broadcast_in_dim.8, s32[256]{0:T(256)S(1)} %bitcast.83, f32[256,16,128]{2,1,0:T(8,128)S(1)} %convolution_multiply_fusion.1), kind=kCustom, calls=%fused_computation.3 | custom fusion | flops 524288 | bytes 6292480 | tf_op jit(solution)/shard_map/scatter-add | solution.py:42
  48.9 0.7 copy-done.1
  49.6 0.0 all-reduce.2.cloned.1.call-update
  49.6 0.1 fusion.16
  49.8 45.6 %all-reduce.2.cloned.1.call-done = f32[8,4,1,16,128]{4,3,1,0,2:T(8,128)} async-done(((f32[8,4,1,16,128]{4,3,1,0,2:T(8,128)}), f32[8,4,1,16,128]{4,3,1,0,2:T(8,128)}) %all-reduce.2.cloned.1.call-update) | async-done | bytes 262160 | tf_op jit(solution)/shard_map/psum | solution.py:45
  95.4 1.5 %dynamic-slice_bitcast_fusion = f32[8,1,1,16,128]{4,3,1,2,0:T(8,128)} fusion(f32[8,4,1,16,128]{4,3,1,0,2:T(8,128)} %all-reduce.2.cloned.1.call-done, s32[]{:T(128)S(6)} %select_n.27), kind=kLoop, calls=%fused_computation.20 | loop fusion | bytes 131076 | tf_op jit(solution)/shard_map/dynamic_slice | solution.py:46
  96.9 4.6 %all-to-all-start = ((f32[8,1,1,16,128]{4,3,1,2,0:T(8,128)}), f32[8,1,1,16,128]{4,3,1,2,0:T(8,128)S(1)}, u32[]{:S(2)}, u32[]{:S(2)}) async-start(f32[8,1,1,16,128]{4,3,1,2,0:T(8,128)} %dynamic-slice_bitcast_fusion), calls=%async_computation | async-start | bytes 131072 | tf_op jit(solution)/shard_map/all_to_all | solution.py:47
  101.5 5.9 %all-to-all-done = f32[8,1,1,16,128]{4,3,1,2,0:T(8,128)S(1)} async-done(((f32[8,1,1,16,128]{4,3,1,2,0:T(8,128)}), f32[8,1,1,16,128]{4,3,1,2,0:T(8,128)S(1)}, u32[]{:S(2)}, u32[]{:S(2)}) %all-to-all-start) | async-done | bytes 65568 | tf_op jit(solution)/shard_map/all_to_all | solution.py:47
  107.4 0.9 multiply_convert_fusion.1
  108.3 0.8 fusion.6
  109.1 3.3 %all-to-all-start.1 = ((bf16[8,1,1,16,128]{4,3,1,2,0:T(8,128)(2,1)}), bf16[8,1,1,16,128]{4,3,1,2,0:T(8,128)(2,1)S(1)}, u32[]{:S(2)}, u32[]{:S(2)}) async-start(bf16[8,1,1,16,128]{4,3,1,2,0:T(8,128)(2,1)} %bitcast.43), calls=%async_computation.1 | async-start | bytes 65536 | tf_op jit(solution)/shard_map/all_to_all | solution.py:64
  112.5 5.7 %all-to-all-done.1 = bf16[8,1,1,16,128]{4,3,1,2,0:T(8,128)(2,1)S(1)} async-done(((bf16[8,1,1,16,128]{4,3,1,2,0:T(8,128)(2,1)}), bf16[8,1,1,16,128]{4,3,1,2,0:T(8,128)(2,1)S(1)}, u32[]{:S(2)}, u32[]{:S(2)}) %all-to-all-start.1) | async-done | bytes 32800 | tf_op jit(solution)/shard_map/all_to_all | solution.py:64
  118.1 8.9 %all_gather.3 = bf16[8,4,1,16,128]{4,3,1,0,2:T(8,128)(2,1)S(1)} all-gather(bf16[8,1,1,16,128]{4,3,1,0,2:T(8,128)(2,1)S(1)} %bitcast.81), channel_id=1, replica_groups=mesh['feat'=8,'col'=4] {'col'}, dimensions={1}, use_global_device_ids=true | all-gather | bytes 163840 | tf_op jit(solution)/shard_map/all_gather | solution.py:65
  127.1 0.8 gather_fusion.1
  127.9 0.0 copy-start.4
  127.9 4.7 %convolution_multiply_fusion = f32[256,16,128]{2,1,0:T(8,128)S(1)} fusion(bf16[256,16,128]{2,1,0:T(8,128)(2,1)S(1)} %gather_fusion.1, bf16[256,128,128]{2,1,0:T(8,128)(2,1)} %param.14, f32[256]{0:T(256)S(1)} %compare_convert_fusion), kind=kOutput, calls=%fused_computation.6 | convolution fusion | flops 134742016 | bytes 11535360 | tf_op jit(solution)/shard_map/nfr,nrk->nfk/dot_general | solution.py:69
  132.6 1.4 fusion.2
  134.0 0.7 copy.30
  (20 shorter events, 0.1 us)
Async XLA Ops:
  7.2 24.3 %copy-start = (bf16[16,4096]{1,0:T(8,128)(2,1)S(1)}, bf16[16,4096]{1,0:T(8,128)(2,1)}, u32[]{:S(2)}) copy-start(bf16[16,4096]{1,0:T(8,128)(2,1)} %param.13) | copy-start | bytes 393220
  7.2 88.2 %all-reduce.2.cloned.1.call-start = ((), (), s32[]{:S(2)}) async-start(), calls=%async_computation.2 | async-start | bytes 524288 | tf_op jit(solution)/shard_map/psum | solution.py:45
  39.9 9.8 %copy-start.2 = (bf16[128,256]{1,0:T(8,128)(2,1)S(1)}, bf16[128,256]{1,0:T(8,128)(2,1)}, u32[]{:S(2)}) copy-start(bf16[128,256]{1,0:T(8,128)(2,1)} %param.20) | copy-start | bytes 196612
  39.9 9.8 %copy-start.3 = (bf16[128,128]{1,0:T(8,128)(2,1)S(1)}, bf16[128,128]{1,0:T(8,128)(2,1)}, u32[]{:S(2)}) copy-start(bf16[128,128]{1,0:T(8,128)(2,1)} %param.12) | copy-start | bytes 98308
  39.9 61.6 %copy-start.8 = (s32[128]{0:T(128)S(1)}, s32[128]{0:T(128)}, u32[]{:S(2)}) copy-start(s32[128]{0:T(128)} %param.19) | copy-start | bytes 1540
  39.9 67.5 %copy-start.5 = (bf16[128,256]{1,0:T(8,128)(2,1)S(1)}, bf16[128,256]{1,0:T(8,128)(2,1)}, u32[]{:S(2)}) copy-start(bf16[128,256]{1,0:T(8,128)(2,1)} %param.21) | copy-start | bytes 196612
  39.9 67.5 %copy-start.7 = (f32[256]{0:T(256)S(1)}, f32[256]{0:T(256)}, u32[]{:S(2)}) copy-start(f32[256]{0:T(256)} %param.22) | copy-start | bytes 3076
  39.9 68.4 %copy-start.6 = (bf16[128,256]{1,0:T(8,128)(2,1)S(1)}, bf16[128,256]{1,0:T(8,128)(2,1)}, u32[]{:S(2)}) copy-start(bf16[128,256]{1,0:T(8,128)(2,1)} %param.23) | copy-start | bytes 196612
  48.9 0.7 copy-start.1
  96.9 10.5 %all-to-all-start = ((f32[8,1,1,16,128]{4,3,1,2,0:T(8,128)}), f32[8,1,1,16,128]{4,3,1,2,0:T(8,128)S(1)}, u32[]{:S(2)}, u32[]{:S(2)}) async-start(f32[8,1,1,16,128]{4,3,1,2,0:T(8,128)} %dynamic-slice_bitcast_fusion), calls=%async_computation | async-start | bytes 131072 | tf_op jit(solution)/shard_map/all_to_all | solution.py:47
  109.1 9.0 %all-to-all-start.1 = ((bf16[8,1,1,16,128]{4,3,1,2,0:T(8,128)(2,1)}), bf16[8,1,1,16,128]{4,3,1,2,0:T(8,128)(2,1)S(1)}, u32[]{:S(2)}, u32[]{:S(2)}) async-start(bf16[8,1,1,16,128]{4,3,1,2,0:T(8,128)(2,1)} %bitcast.43), calls=%async_computation.1 | async-start | bytes 65536 | tf_op jit(solution)/shard_map/all_to_all | solution.py:64
  127.9 4.7 %copy-start.4 = (s32[256]{0:T(256)S(1)}, s32[256]{0:T(256)}, u32[]{:S(2)}) copy-start(s32[256]{0:T(256)} %param.16) | copy-start | bytes 3076
Sparse Core Ops, SparseCore 0:
  49.7 45.6 all-reduce.1
where the time goes:
time: 142 us
  waiting for transfers between devices  57.2 us (40%)
  other arithmetic  31.1 us (22%)
  between operations  14.9 us (10%)
  matrix products  14.7 us (10%)
  blocking collectives  8.92 us (6%)
  starting transfers between devices  7.98 us (6%)
  local copies, waits for them, and re-layouts  6.79 us (5%)
    psum x1, waiting for transfers between devices, local(): total = lax.psum(grid, 'col')  45.6 us
    gather x1, other arithmetic, local(): target = places[tile_rows]  20.7 us
    scatter-add x1, other arithmetic, local(): jnp.zeros((blocks_total, slice_width, tile_size), jnp.float32).at[target]  8.97 us
    all_gather x1, blocking collectives, local(): everything = lax.all_gather(regrouped, 'col', axis=1, tiled=True)  8.92 us
    dot_general x1, matrix products, local(): jnp.einsum('nfk,nrk->nfr', picked, tiles, preferred_element_type=jnp.floa...  6.77 us
    all_to_all x1, waiting for transfers between devices, local(): lax.all_to_all(mine, 'feat', split_axis=0, concat_axis=1, tiled=True)  5.9 us
    all_to_all x1, waiting for transfers between devices, local(): lax.all_to_all(arranged, 'feat', split_axis=0, concat_axis=0, tiled=True)  5.66 us
    dot_general x1, matrix products, local(): jnp.einsum('nfr,nrk->nfk', taken, tiles, preferred_element_type=jnp.float32)  4.68 us
  transfers between devices with their start and end apart: 3, of which 3 were waited for; matrix products, arithmetic and copies ran while one was open for 0% of the time, Pallas kernels for 0%

commit v1 on v0

--- a/solution.py
+++ b/solution.py
@@ -62,7 +62,14 @@
     arranged = back.reshape(row_blocks, tile_size, nfeat, slice_width).transpose(2, 0, 3, 1)
     arranged = arranged.reshape(nfeat, 1, row_blocks, slice_width, tile_size)
     regrouped = lax.all_to_all(arranged, "feat", split_axis=0, concat_axis=0, tiled=True)
-    everything = lax.all_gather(regrouped, "col", axis=1, tiled=True)
+    size = lax.axis_size("col")
+    right = [(i, (i + 1) % size) for i in range(size)]
+    parts = [regrouped]
+    for far in range(1, size):
+        parts = [lax.ppermute(parts[0], "col", right), *parts]
+    result = jnp.concatenate(parts, axis=1)
+    places_2 = (lax.axis_index("col") + 1) * parts[-1].shape[1]
+    everything = jnp.roll(result, places_2, axis=1)
     row_grads = everything.reshape(blocks_total, slice_width, tile_size)
     taken = row_grads[target]
     pieces = (

time: 142 us -> 146 us (1.028)
  waiting for transfers between devices: 57.2 us -> 63.9 us
    ppermute x0 -> x3, waiting for transfers between devices: none -> 12.4 us  [local(): parts = [lax.ppermute(parts[0], 'col', right), *parts]]
    all_gather x1 -> x0, blocking collectives: 8.92 us -> none  [local(): everything = lax.all_gather(regrouped, 'col', axis=1, tiled=True)]
    all_to_all x0 -> x1, blocking collectives: none -> 8.12 us  [local(): lax.all_to_all(arranged, 'feat', split_axis=0, concat_axis=0, tiled=True)]
    all_to_all x1 -> x0, waiting for transfers between devices: 5.66 us -> none  [local(): lax.all_to_all(arranged, 'feat', split_axis=0, concat_axis=0, tiled=True)]
    all_to_all x1 -> x0, starting transfers between devices: 3.34 us -> none  [local(): lax.all_to_all(arranged, 'feat', split_axis=0, concat_axis=0, tiled=True)]
    ppermute x0 -> x3, starting transfers between devices: none -> 2.02 us  [local(): parts = [lax.ppermute(parts[0], 'col', right), *parts]]
  transfers between devices with their start and end apart: 3 -> 5, of which waited for: 3 -> 5; matrix products, arithmetic and copies ran while one was open for 0% -> 0% of each run, Pallas kernels for 0% -> 0%
where the time goes in v1:
time: 146 us
  waiting for transfers between devices  63.9 us (44%)
  other arithmetic  31.1 us (21%)
  between operations  15 us (10%)
  matrix products  14 us (10%)
  blocking collectives  8.12 us (6%)
  local copies, waits for them, and re-layouts  6.9 us (5%)
  starting transfers between devices  6.66 us (5%)
    psum x1, waiting for transfers between devices, local(): total = lax.psum(grid, 'col')  45.6 us
    gather x1, other arithmetic, local(): target = places[tile_rows]  20.8 us
    ppermute x3, waiting for transfers between devices, local(): parts = [lax.ppermute(parts[0], 'col', right), *parts]  12.4 us
    scatter-add x1, other arithmetic, local(): jnp.zeros((blocks_total, slice_width, tile_size), jnp.float32).at[target]  8.97 us
    all_to_all x1, blocking collectives, local(): lax.all_to_all(arranged, 'feat', split_axis=0, concat_axis=0, tiled=True)  8.12 us
    dot_general x1, matrix products, local(): jnp.einsum('nfk,nrk->nfr', picked, tiles, preferred_element_type=jnp.floa...  6.77 us
    all_to_all x1, waiting for transfers between devices, local(): lax.all_to_all(mine, 'feat', split_axis=0, concat_axis=1, tiled=True)  5.9 us
    dot_general x1, matrix products, local(): jnp.einsum('nfr,nrk->nfk', taken, tiles, preferred_element_type=jnp.float32)  4.68 us
  transfers between devices with their start and end apart: 5, of which 5 were waited for; matrix products, arithmetic and copies ran while one was open for 0% of the time, Pallas kernels for 0%

profile of v1, /device:TPU:0, one launch (start us, length us, event | category | flops | bytes accessed | tf_op | source)
XLA Modules:
  0.0 145.7 jit_solution(14342107557298035952)
XLA Ops:
  7.2 0.0 copy-start
  7.2 0.0 all-reduce.2.cloned.1.call-start
  7.2 0.7 compare_select_fusion.3
  7.9 0.7 scatter_custom_fusion
  8.6 0.7 fusion.14
  9.3 0.7 fusion.15
  10.0 20.8 %compare_select_fusion.4 = s32[256]{0:T(256)S(1)} fusion(s32[256]{0:T(256)} %param.15, s32[]{:T(128)} %bitcast, s32[]{:T(128)} %bitcast.1, s32[]{:T(128)} %bitcast.2, s32[]{:T(128)} %bitcast.3, s32[]{:T(128)} %bitcast.4, s32[]{:T(128)} %bitcast.5, s32[]{:T(128)} %bitcast.6, s32[]{:T(128)} %bitcast.7, s32[]{:T(128)} %bitcast.8, s32[]{:T(128)} %bitcast.9, ...), kind=kLoop, calls=%fused_computation.38 | loop fusion | flops 16640 | bytes 2176 | tf_op jit(solution)/shard_map/gather | solution.py:33
  31.5 0.7 compare_select_fusion.1
  32.2 0.8 gather_fusion
  33.1 6.8 %convolution_multiply_fusion.1 = f32[256,16,128]{2,1,0:T(8,128)S(1)} fusion(bf16[256,16,128]{2,1,0:T(8,128)(2,1)S(1)} %gather_fusion, bf16[256,128,128]{2,1,0:T(8,128)(2,1)} %param.14, f32[256]{0:T(256)S(1)} %compare_convert_fusion), kind=kOutput, calls=%fused_computation.7 | convolution fusion | flops 134742016 | bytes 11535360 | tf_op jit(solution)/shard_map/nfk,nrk->nfr/dot_general | solution.py:38
  39.9 0.0 copy-start.2
  39.9 0.0 copy-start.3
  39.9 9.0 %scatter_fusion = f32[32,16,128]{2,1,0:T(8,128)S(1)} fusion(f32[32,16,128]{2,1,0:T(8,128)S(1)} %broadcast_in_dim.8, s32[256]{0:T(256)S(1)} %bitcast.88, f32[256,16,128]{2,1,0:T(8,128)S(1)} %convolution_multiply_fusion.1), kind=kCustom, calls=%fused_computation.3 | custom fusion | flops 524288 | bytes 6292480 | tf_op jit(solution)/shard_map/scatter-add | solution.py:42
  48.9 0.7 copy-done.1
  49.6 0.0 all-reduce.2.cloned.1.call-update
  49.7 0.1 fusion.16
  49.8 45.6 %all-reduce.2.cloned.1.call-done = f32[8,4,1,16,128]{4,3,1,0,2:T(8,128)} async-done(((f32[8,4,1,16,128]{4,3,1,0,2:T(8,128)}), f32[8,4,1,16,128]{4,3,1,0,2:T(8,128)}) %all-reduce.2.cloned.1.call-update) | async-done | bytes 262160 | tf_op jit(solution)/shard_map/psum | solution.py:45
  95.5 1.5 %dynamic-slice_bitcast_fusion = f32[8,1,1,16,128]{4,3,1,2,0:T(8,128)} fusion(f32[8,4,1,16,128]{4,3,1,0,2:T(8,128)} %all-reduce.2.cloned.1.call-done, s32[]{:T(128)S(6)} %select_n.40), kind=kLoop, calls=%fused_computation.20 | loop fusion | bytes 131076 | tf_op jit(solution)/shard_map/dynamic_slice | solution.py:46
  96.9 4.6 %all-to-all-start = ((f32[8,1,1,16,128]{4,3,1,2,0:T(8,128)}), f32[8,1,1,16,128]{4,3,1,2,0:T(8,128)S(1)}, u32[]{:S(2)}, u32[]{:S(2)}) async-start(f32[8,1,1,16,128]{4,3,1,2,0:T(8,128)} %dynamic-slice_bitcast_fusion), calls=%async_computation | async-start | bytes 131072 | tf_op jit(solution)/shard_map/all_to_all | solution.py:47
  101.6 5.9 %all-to-all-done = f32[8,1,1,16,128]{4,3,1,2,0:T(8,128)S(1)} async-done(((f32[8,1,1,16,128]{4,3,1,2,0:T(8,128)}), f32[8,1,1,16,128]{4,3,1,2,0:T(8,128)S(1)}, u32[]{:S(2)}, u32[]{:S(2)}) %all-to-all-start) | async-done | bytes 65568 | tf_op jit(solution)/shard_map/all_to_all | solution.py:47
  107.5 0.9 multiply_convert_fusion.1
  108.3 0.2 fusion.6
  108.5 8.1 %all_to_all.14 = bf16[8,1,1,16,128]{4,3,1,2,0:T(8,128)(2,1)S(1)} all-to-all(bf16[8,1,1,16,128]{4,3,1,2,0:T(8,128)(2,1)S(1)} %bitcast.87), channel_id=1, replica_groups=mesh['feat'=8,'col'=4] {'feat'}, dimensions={0} | all-to-all | bytes 65536 | tf_op jit(solution)/shard_map/all_to_all | solution.py:64
  116.7 1.5 collective-permute-start
  118.1 3.4 %collective-permute-done = bf16[8,1,1,16,128]{4,3,1,0,2:T(8,128)(2,1)S(1)} collective-permute-done((bf16[8,1,1,16,128]{4,3,1,0,2:T(8,128)(2,1)S(1)}, bf16[8,1,1,16,128]{4,3,1,0,2:T(8,128)(2,1)S(1)}, u32[]{:S(2)}, u32[]{:S(2)}) %collective-permute-start) | collective-permute-done | bytes 32800 | tf_op jit(solution)/shard_map/ppermute | solution.py:69
  121.5 0.6 collective-permute-start.1
  122.0 4.3 %collective-permute-done.1 = bf16[8,1,1,16,128]{4,3,1,0,2:T(8,128)(2,1)S(1)} collective-permute-done((bf16[8,1,1,16,128]{4,3,1,0,2:T(8,128)(2,1)S(1)}, bf16[8,1,1,16,128]{4,3,1,0,2:T(8,128)(2,1)S(1)}, u32[]{:S(2)}, u32[]{:S(2)}) %collective-permute-start.1) | collective-permute-done | bytes 32800 | tf_op jit(solution)/shard_map/ppermute | solution.py:69
  126.3 4.8 %collective-permute-done.2 = bf16[8,1,1,16,128]{4,3,1,0,2:T(8,128)(2,1)S(1)} collective-permute-done((bf16[8,1,1,16,128]{4,3,1,0,2:T(8,128)(2,1)S(1)}, bf16[8,1,1,16,128]{4,3,1,0,2:T(8,128)(2,1)S(1)}, u32[]{:S(2)}, u32[]{:S(2)}) %collective-permute-start.2) | collective-permute-done | bytes 32800 | tf_op jit(solution)/shard_map/ppermute | solution.py:69
  131.2 0.9 gather_fusion.1
  132.1 4.7 %convolution_multiply_fusion = f32[256,16,128]{2,1,0:T(8,128)S(1)} fusion(bf16[256,16,128]{2,1,0:T(8,128)(2,1)S(1)} %gather_fusion.1, bf16[256,128,128]{2,1,0:T(8,128)(2,1)} %param.14, f32[256]{0:T(256)S(1)} %compare_convert_fusion), kind=kOutput, calls=%fused_computation.6 | convolution fusion | flops 134742016 | bytes 11535360 | tf_op jit(solution)/shard_map/nfr,nrk->nfk/dot_general | solution.py:76
  136.8 1.4 fusion.2
  138.2 0.7 copy.32
  (33 shorter events, 0.2 us)
Async XLA Ops:
  7.2 24.3 %copy-start = (bf16[16,4096]{1,0:T(8,128)(2,1)S(1)}, bf16[16,4096]{1,0:T(8,128)(2,1)}, u32[]{:S(2)}) copy-start(bf16[16,4096]{1,0:T(8,128)(2,1)} %param.13) | copy-start | bytes 393220
  7.2 88.3 %all-reduce.2.cloned.1.call-start = ((), (), s32[]{:S(2)}) async-start(), calls=%async_computation.2 | async-start | bytes 524288 | tf_op jit(solution)/shard_map/psum | solution.py:45
  39.9 9.8 %copy-start.2 = (bf16[128,256]{1,0:T(8,128)(2,1)S(1)}, bf16[128,256]{1,0:T(8,128)(2,1)}, u32[]{:S(2)}) copy-start(bf16[128,256]{1,0:T(8,128)(2,1)} %param.20) | copy-start | bytes 196612
  39.9 9.8 %copy-start.3 = (bf16[128,128]{1,0:T(8,128)(2,1)S(1)}, bf16[128,128]{1,0:T(8,128)(2,1)}, u32[]{:S(2)}) copy-start(bf16[128,128]{1,0:T(8,128)(2,1)} %param.12) | copy-start | bytes 98308
  39.9 61.6 %copy-start.8 = (s32[128]{0:T(128)S(1)}, s32[128]{0:T(128)}, u32[]{:S(2)}) copy-start(s32[128]{0:T(128)} %param.19) | copy-start | bytes 1540
  39.9 67.6 %copy-start.5 = (bf16[128,256]{1,0:T(8,128)(2,1)S(1)}, bf16[128,256]{1,0:T(8,128)(2,1)}, u32[]{:S(2)}) copy-start(bf16[128,256]{1,0:T(8,128)(2,1)} %param.21) | copy-start | bytes 196612
  39.9 67.6 %copy-start.7 = (f32[256]{0:T(256)S(1)}, f32[256]{0:T(256)}, u32[]{:S(2)}) copy-start(f32[256]{0:T(256)} %param.22) | copy-start | bytes 3076
  39.9 68.4 %copy-start.6 = (bf16[128,256]{1,0:T(8,128)(2,1)S(1)}, bf16[128,256]{1,0:T(8,128)(2,1)}, u32[]{:S(2)}) copy-start(bf16[128,256]{1,0:T(8,128)(2,1)} %param.23) | copy-start | bytes 196612
  48.9 0.7 copy-start.1
  96.9 10.5 %all-to-all-start = ((f32[8,1,1,16,128]{4,3,1,2,0:T(8,128)}), f32[8,1,1,16,128]{4,3,1,2,0:T(8,128)S(1)}, u32[]{:S(2)}, u32[]{:S(2)}) async-start(f32[8,1,1,16,128]{4,3,1,2,0:T(8,128)} %dynamic-slice_bitcast_fusion), calls=%async_computation | async-start | bytes 131072 | tf_op jit(solution)/shard_map/all_to_all | solution.py:47
  116.7 4.8 %collective-permute-start = (bf16[8,1,1,16,128]{4,3,1,0,2:T(8,128)(2,1)S(1)}, bf16[8,1,1,16,128]{4,3,1,0,2:T(8,128)(2,1)S(1)}, u32[]{:S(2)}, u32[]{:S(2)}) collective-permute-start(bf16[8,1,1,16,128]{4,3,1,0,2:T(8,128)(2,1)S(1)} %bitcast.85), channel_id=1, source_target_pairs={{0,1},{1,2},{2,3},{3,0},{4,5},{5,6},{6,7},{7,4},{8,9},{9,10},{10,1... | collective-permute-start | bytes 98312 | tf_op jit(solution)/shard_map/ppermute | solution.py:69
  121.5 4.8 %collective-permute-start.1 = (bf16[8,1,1,16,128]{4,3,1,0,2:T(8,128)(2,1)S(1)}, bf16[8,1,1,16,128]{4,3,1,0,2:T(8,128)(2,1)S(1)}, u32[]{:S(2)}, u32[]{:S(2)}) collective-permute-start(bf16[8,1,1,16,128]{4,3,1,0,2:T(8,128)(2,1)S(1)} %collective-permute-done), channel_id=1, source_target_pairs={{0,1},{1,2},{2,3},{3,0},{4,5},{5,6},{6,7},{7,4},{8,9},{9,10},{10,1... | collective-permute-start | bytes 98312 | tf_op jit(solution)/shard_map/ppermute | solution.py:69
  126.3 4.8 %collective-permute-start.2 = (bf16[8,1,1,16,128]{4,3,1,0,2:T(8,128)(2,1)S(1)}, bf16[8,1,1,16,128]{4,3,1,0,2:T(8,128)(2,1)S(1)}, u32[]{:S(2)}, u32[]{:S(2)}) collective-permute-start(bf16[8,1,1,16,128]{4,3,1,0,2:T(8,128)(2,1)S(1)} %collective-permute-done.1), channel_id=1, source_target_pairs={{0,1},{1,2},{2,3},{3,0},{4,5},{5,6},{6,7},{7,4},{8,9},{9,10},{10,1... | collective-permute-start | bytes 98312 | tf_op jit(solution)/shard_map/ppermute | solution.py:69
  132.1 4.7 %copy-start.4 = (s32[256]{0:T(256)S(1)}, s32[256]{0:T(256)}, u32[]{:S(2)}) copy-start(s32[256]{0:T(256)} %param.16) | copy-start | bytes 3076
Sparse Core Ops, SparseCore 0:
  49.8 45.6 all-reduce.1
